TPU v7x, 512 devices: a whole 4x4x16 slice. The times are simulated.
512 devices in a mesh: segment: 32 (over z, core), head: 16 (over y, x).
Axes of the slice: x: 4, y: 4, z: 16, core: 2. Of those that a mesh axis runs over, the one named last changes fastest.
Arguments:
- slices: bfloat16 [4096, 4096], P('segment', 'head'), may hold values from -6 to 6
- new_slice: bfloat16 [128, 4096], P(None, 'head'), may hold values from -6 to 6
- norm_gain: float32 [32, 4096], P('segment'), may hold values from 0.1 to 1.9
- w_query: bfloat16 [32, 4096, 2048], P('segment', None, 'head'), may hold values from -0.09375 to 0.09375
- w_keyval: bfloat16 [32, 4096, 1024], P('segment', None, 'head'), may hold values from -0.1875 to 0.1875
- w_out: bfloat16 [32, 2048, 4096], P('segment', 'head'), may hold values from -0.375 to 0.375
- cached_rows: bfloat16 [32, 16384, 256], P('segment', 'head'), may hold values from -400 to 400
- lengths: int32 [32], P('segment'), may hold values from 256 to 4096
Outputs:
- first_pass: float32 [4096, 4096], P('segment', 'head')
- second_pass: float32 [4096, 4096], P('segment', 'head')
All inputs are finite; a program needn't handle non-finite values.
Results may differ from a plain program's by a relative error of at most 0.029.
The roundings to bfloat16 on the way count: a program that leaves them out, or rounds other values in their place, can miss the bound.
Values may be sent and summed in bfloat16 or wider, within the bound.
No kernel may reach another device: no remote copies, remote signals or barrier semaphores. Data moves between devices by JAX's collectives and lax.ppermute only.
A program may use at most 64 MiB of HBM per device.

v0:
```python
import jax
import jax.numpy as jnp
from jax import lax
from jax.sharding import PartitionSpec as P

KVH = 4
HD = 128


EPSILON = 1e-05
ROPE_BASE = 1000000.0
NEGATIVE = -1e30


def swapped(block, axis, bit):
    count = lax.axis_size(axis)
    route = []
    for low in range(count):
        high = low | 1 << bit
        if high != low and high < count:
            route += [(low, high), (high, low)]
    return lax.ppermute(block, axis, route)


def from_behind(shard, axis, by):
    peers = lax.axis_size(axis)
    pairs = [(i, i + by) for i in range(peers) if 0 <= i + by < peers]
    return lax.ppermute(shard, axis, pairs)


def rotate(entries, positions):
    half_dim = entries.shape[-1] // 2
    exponent = jnp.arange(half_dim, dtype=jnp.float32) * (2.0 / entries.shape[-1])
    inverse = jnp.power(jnp.float32(ROPE_BASE), -exponent)
    angles = positions[:, None] * inverse[None, :]
    cosine = jnp.cos(angles)[:, None, :]
    sine = jnp.sin(angles)[:, None, :]
    first_half = entries[..., :half_dim]
    second_half = entries[..., half_dim:]
    return jnp.concatenate(
        [first_half * cosine - second_half * sine, second_half * cosine + first_half * sine],
        axis=-1,
    )


def normalize(rows_in, gain_vector):
    mean_square = jnp.mean(rows_in * rows_in, axis=-1, keepdims=True)
    return (rows_in * lax.rsqrt(mean_square + EPSILON) * gain_vector).astype(jnp.bfloat16)


def combine_partial(left_side, right_side):
    left_peak, left_total, left_out = left_side
    right_peak, right_total, right_out = right_side
    joined = jnp.maximum(left_peak, right_peak)
    left_scale = jnp.exp(left_peak - joined)
    right_scale = jnp.exp(right_peak - joined)
    return (
        joined,
        left_scale * left_total + right_scale * right_total,
        left_scale[..., None] * left_out + right_scale[..., None] * right_out,
    )


def softmax_partial(queries, key_rows, value_rows, visible):
    scores = jnp.einsum(
        "rnd,kd->nrk", queries, key_rows, preferred_element_type=jnp.float32
    ) * HD ** (-0.5)
    scores = jnp.where(visible[None], scores, NEGATIVE)
    row_peak = jnp.max(scores, axis=-1)
    weights = jnp.where(visible[None], jnp.exp(scores - row_peak[..., None]), 0.0)
    row_total = jnp.sum(weights, axis=-1)
    outputs = jnp.einsum(
        "nrk,kd->nrd", weights.astype(jnp.bfloat16), value_rows, preferred_element_type=jnp.float32
    )
    return (row_peak, row_total, outputs)


def blank_partial(head_total, row_total):
    return (
        jnp.full((head_total, row_total), NEGATIVE, jnp.float32),
        jnp.zeros((head_total, row_total), jnp.float32),
        jnp.zeros((head_total, row_total, HD), jnp.float32),
    )


def attend_range(query_set, key_table, low_bound, high_bound, block_rows):
    row_total = query_set.shape[0]
    first_block = low_bound // block_rows
    last_block = (high_bound + block_rows - 1) // block_rows

    def one_block(turn_index, running):
        block_start = (first_block + turn_index) * block_rows
        key_piece = lax.dynamic_slice_in_dim(key_table, block_start, block_rows, 0)
        places = block_start + jnp.arange(block_rows, dtype=jnp.int32)
        live_mask = (places >= low_bound) & (places < high_bound)
        visible = jnp.broadcast_to(live_mask[None, :], (row_total, block_rows))
        return combine_partial(
            running, softmax_partial(query_set, key_piece[:, :HD], key_piece[:, HD:], visible)
        )

    turns = jnp.maximum(last_block - first_block, 0)
    return lax.fori_loop(0, turns, one_block, blank_partial(query_set.shape[1], row_total))


def local(slices, new_slice, norm_gain, w_query, w_keyval, w_out, cached_rows, lengths):
    segment_index = lax.axis_index("segment")
    head_index = lax.axis_index("head")
    head_count = lax.axis_size("head")
    row_count, width = slices.shape
    group_size = head_count // KVH
    bit_count = group_size.bit_length() - 1
    position = head_index % group_size
    local_heads = w_query.shape[2] // HD
    length = lengths[0]
    gain_vector = norm_gain[0]
    query_w = w_query[0]
    keyval_w = w_keyval[0]
    out_w = w_out[0]
    cache_rows = cached_rows[0]
    row_ids = jnp.arange(row_count, dtype=jnp.int32)
    causal = row_ids[:, None] >= row_ids[None, :]
    assembled = cache_rows
    for bit_number in range(bit_count):
        partner_rows = swapped(assembled, "head", bit_number)
        high_bit = position // (1 << bit_number) % 2
        assembled = jnp.where(
            high_bit == 0,
            jnp.concatenate([assembled, partner_rows], axis=0),
            jnp.concatenate([partner_rows, assembled], axis=0),
        )
    table_rows = assembled.shape[0]
    block_rows = min(512, table_rows // 4)
    own_live = jnp.clip(length, 0, table_rows)

    def cache_partial(query_set):
        combined = attend_range(query_set, assembled, 0, own_live, block_rows)
        return combined

    def project(full_rows, offset):
        normed = normalize(full_rows, gain_vector)
        positions = (length + offset + row_ids).astype(jnp.float32)
        queries = jnp.dot(normed, query_w, preferred_element_type=jnp.float32).reshape(
            row_count, local_heads, HD
        )
        queries = rotate(queries, positions).astype(jnp.bfloat16)
        chosen = jnp.dot(normed, keyval_w, preferred_element_type=jnp.float32)
        for bit_number in range(bit_count):
            partner_part = swapped(chosen, "head", bit_number)
            high_bit = position // (1 << bit_number) % 2
            chosen = jnp.where(
                high_bit == 0,
                jnp.concatenate([chosen, partner_part], axis=1),
                jnp.concatenate([partner_part, chosen], axis=1),
            )
        new_keys = rotate(chosen[:, None, :HD], positions)[:, 0].astype(jnp.bfloat16)
        new_values = chosen[:, HD:].astype(jnp.bfloat16)
        return (queries, new_keys, new_values)

    def attend(queries, new_keys, new_values, earlier):
        if earlier is None:
            recent_keys = new_keys
            recent_values = new_values
            recent_live = causal
        else:
            recent_keys = jnp.concatenate([earlier[0], new_keys], axis=0)
            recent_values = jnp.concatenate([earlier[1], new_values], axis=0)
            recent_live = jnp.concatenate([jnp.ones((row_count, row_count), bool), causal], axis=1)
        running = cache_partial(queries)
        recent = softmax_partial(queries, recent_keys, recent_values, recent_live)
        row_peak, row_total, outputs = combine_partial(running, recent)
        attended = (outputs / row_total[..., None]).astype(jnp.bfloat16).transpose(1, 0, 2)
        return attended.reshape(row_count, local_heads * HD)

    def mix(full_rows, offset, earlier):
        queries, new_keys, new_values = project(full_rows, offset)
        attended = attend(queries, new_keys, new_values, earlier)
        return (
            jnp.dot(attended, out_w, preferred_element_type=jnp.float32),
            (new_keys, new_values),
        )

    def advance(own_rows, offset, earlier):
        full_rows = lax.all_gather(own_rows, "head", axis=1, tiled=True)
        partial_out, recent = mix(full_rows, offset, earlier)
        summed = lax.psum_scatter(partial_out, "head", scatter_dimension=1, tiled=True)
        return (own_rows + summed, recent)

    first_out, recent = advance(slices.astype(jnp.float32), 0, None)
    arrived = from_behind(first_out, "segment", 1)
    entering = jnp.where(segment_index == 0, new_slice.astype(jnp.float32), arrived)
    second_out, _ = advance(entering, row_count, recent)
    return (first_out, second_out)


def solution(mesh):
    placed = (
        P("segment", "head"),
        P(None, "head"),
        P("segment", None),
        P("segment", None, "head"),
        P("segment", None, "head"),
        P("segment", "head", None),
        P("segment", "head", None),
        P("segment"),
    )
    return jax.shard_map(
        local,
        mesh=mesh,
        in_specs=placed,
        out_specs=(P("segment", "head"), P("segment", "head")),
        check_vma=False,
    )
```

profile of v0, /device:TPU:2, one launch (start us, length us, event | category | flops | bytes accessed | tf_op | source)
XLA Modules:
  0.0 417.6 jit_solution(12259424479414323650)
XLA Ops:
  7.2 1.6 convert_element_type.74
  8.9 7.8 %collective-permute-start = (bf16[1024,256]{1,0:T(8,128)(2,1)}, bf16[1024,256]{1,0:T(8,128)(2,1)S(1)}, u32[]{:S(2)}, u32[]{:S(2)}) collective-permute-start(bf16[1024,256]{1,0:T(8,128)(2,1)} %bitcast.245), channel_id=1, source_target_pairs={{0,1},{1,0},{2,3},{3,2},{4,5},{5,4},{6,7},{7,6},{8,9},{9,8},{10,11... | collective-permute-start | bytes 1572872 | tf_op jit(solution)/shard_map/ppermute | solution.py:22
  16.7 7.9 %collective-permute-done = bf16[1024,256]{1,0:T(8,128)(2,1)S(1)} collective-permute-done((bf16[1024,256]{1,0:T(8,128)(2,1)}, bf16[1024,256]{1,0:T(8,128)(2,1)S(1)}, u32[]{:S(2)}, u32[]{:S(2)}) %collective-permute-start) | collective-permute-done | bytes 524320 | tf_op jit(solution)/shard_map/ppermute | solution.py:22
  24.7 1.5 maximum_select_fusion.1
  26.1 4.0 collective-permute-start.1
  30.9 61.6 %all-gather.3.cloned.1.call-done = f32[128,4096]{1,0:T(8,128)} async-done(((f32[128,256]{1,0:T(8,128)}), f32[128,4096]{1,0:T(8,128)}) %all-gather.3.cloned.1.call-update) | async-done | bytes 2097168 | tf_op jit(solution)/shard_map/all_gather | solution.py:183
  92.6 2.0 multiply_reduce_fusion.1
  95.4 2.9 collective-permute-start.2
  98.3 2.7 maximum_select_fusion
  101.3 4.0 collective-permute-start.3
  106.0 3.0 collective-permute-done.3
  109.4 1.7 while.28
  111.4 1.9 fusion.54
  113.4 94.4 %reduce-scatter.3.cloned.1.call-done = f32[128,256]{1,0:T(8,128)} async-done(((f32[128,4096]{1,0:T(8,128)}), f32[128,256]{1,0:T(8,128)}) %reduce-scatter.3.cloned.1.call-update) | async-done | bytes 131088 | tf_op jit(solution)/shard_map/reduce_scatter | solution.py:185
  208.7 1.3 collective-permute-start.4
  210.0 1.0 collective-permute-done.4
  211.8 67.0 %all-gather.5.cloned.1.call-done = f32[128,4096]{1,0:T(8,128)} async-done(((f32[128,256]{1,0:T(8,128)}), f32[128,4096]{1,0:T(8,128)}) %all-gather.5.cloned.1.call-update) | async-done | bytes 2097168 | tf_op jit(solution)/shard_map/all_gather | solution.py:183
  278.8 2.0 multiply_reduce_fusion
  281.0 1.6 fusion.58
  282.6 2.8 collective-permute-start.5
  285.4 3.0 collective-permute-done.5
  288.5 4.0 collective-permute-start.6
  292.5 1.8 convolution_bitcast_fusion
  294.3 1.9 collective-permute-done.6
  296.6 5.3 %while.29 = (s32[]{:T(128)}, f32[1,128]{1,0:T(1,128)S(1)}, f32[1,128]{1,0:T(1,128)S(1)}, f32[1,128,128]{2,1,0:T(8,128)S(1)}, s32[]{:T(128)}, /*index=5*/s32[]{:T...) while((s32[]{:T(128)}, f32[1,128]{1,0:T(1,128)S(1)}, ...), condition=%wide.region_12.13_spmd, body=%wide.region_9.12_spmd.sunk | while | flops 34196100 | bytes 1224395 | solution.py:102
  296.6 1.1 fusion.196
  298.0 1.3 fusion.200
  299.3 1.2 fusion.196
  300.6 1.3 fusion.200
  302.2 1.9 fusion.52
  304.2 105.3 %reduce-scatter.5.cloned.1.call-done = f32[128,256]{1,0:T(8,128)} async-done(((f32[128,4096]{1,0:T(8,128)}), f32[128,256]{1,0:T(8,128)}) %reduce-scatter.5.cloned.1.call-update) | async-done | bytes 131088 | tf_op jit(solution)/shard_map/reduce_scatter | solution.py:185
  409.5 1.6 add.150
  (99 shorter events, 7.1 us)
Async XLA Ops:
  7.2 104.2 %copy-start = (bf16[1,128,4096]{2,1,0:T(8,128)(2,1)S(1)}, bf16[1,128,4096]{2,1,0:T(8,128)(2,1)}, u32[]{:S(2)}) copy-start(bf16[1,128,4096]{2,1,0:T(8,128)(2,1)} %param.17) | copy-start | bytes 3145732
  7.2 85.4 %all-gather.3.cloned.1.call-start = ((), (), s32[]{:S(2)}) async-start(), calls=%async_computation.2 | async-start | bytes 2228224 | tf_op jit(solution)/shard_map/all_gather | solution.py:183
  8.8 199.0 %reduce-scatter.3.cloned.1.call-start = ((), (), s32[]{:S(2)}) async-start(), calls=%async_computation.3 | async-start | bytes 2228224 | tf_op jit(solution)/shard_map/reduce_scatter | solution.py:185
  8.9 15.8 %collective-permute-start = (bf16[1024,256]{1,0:T(8,128)(2,1)}, bf16[1024,256]{1,0:T(8,128)(2,1)S(1)}, u32[]{:S(2)}, u32[]{:S(2)}) collective-permute-start(bf16[1024,256]{1,0:T(8,128)(2,1)} %bitcast.245), channel_id=1, source_target_pairs={{0,1},{1,0},{2,3},{3,2},{4,5},{5,4},{6,7},{7,6},{8,9},{9,8},{10,11... | collective-permute-start | bytes 1572872 | tf_op jit(solution)/shard_map/ppermute | solution.py:22
  16.7 77.8 %copy-start.6 = (bf16[1,4096,64]{1,2,0:T(8,128)(2,1)S(1)}, bf16[1,4096,64]{1,2,0:T(8,128)(2,1)}, u32[]{:S(2)}) copy-start(bf16[1,4096,64]{1,2,0:T(8,128)(2,1)} %param.16) | copy-start | bytes 1572868
  16.7 77.8 %copy-start.8 = (f32[1,4096]{1,0:T(1,128)S(1)}, f32[1,4096]{1,0:T(1,128)}, u32[]{:S(2)}) copy-start(f32[1,4096]{1,0:T(1,128)} %param.14) | copy-start | bytes 49156
  26.1 69.2 %copy-start.4 = (bf16[2048,256]{1,0:T(8,128)(2,1)}, bf16[2048,256]{1,0:T(8,128)(2,1)S(1)}, u32[]{:S(2)}) copy-start(bf16[2048,256]{1,0:T(8,128)(2,1)S(1)} %maximum_select_fusion.1) | copy-start | bytes 3145732
  26.1 72.2 %collective-permute-start.1 = (bf16[2048,256]{1,0:T(8,128)(2,1)S(1)}, bf16[2048,256]{1,0:T(8,128)(2,1)}, u32[]{:S(2)}, u32[]{:S(2)}) collective-permute-start(bf16[2048,256]{1,0:T(8,128)(2,1)S(1)} %maximum_select_fusion.1), channel_id=1, source_target_pairs={{0,2},{2,0},{1,3},{3,1},{4,6},{6,4},{5,7},{7,5},{8,10},{10,8},{9,1... | collective-permute-start | bytes 3145736 | tf_op jit(solution)/shard_map/ppermute | solution.py:22
  30.9 78.1 %copy-start.12 = (f32[64]{0:T(128)}, f32[64]{0:T(128)S(1)}, u32[]{:S(2)}) copy-start(f32[64]{0:T(128)S(1)} %negate_power_fusion) | copy-start | bytes 772
  92.6 2.2 copy-start.1
  95.4 10.0 %copy-start.5 = (bf16[1,4096,128]{2,1,0:T(8,128)(2,1)S(1)}, bf16[1,4096,128]{2,1,0:T(8,128)(2,1)}, u32[]{:S(2)}) copy-start(bf16[1,4096,128]{2,1,0:T(8,128)(2,1)} %param.15) | copy-start | bytes 3145732
  95.4 5.9 %collective-permute-start.2 = (f32[128,64]{0,1:T(8,128)S(1)}, f32[128,64]{0,1:T(8,128)S(1)}, u32[]{:S(2)}, u32[]{:S(2)}) collective-permute-start(f32[128,64]{0,1:T(8,128)S(1)} %fusion.60), channel_id=1, source_target_pairs={{0,1},{1,0},{2,3},{3,2},{4,5},{5,4},{6,7},{7,6},{8,9},{9,8},{10,11... | collective-permute-start | bytes 98312 | tf_op jit(solution)/shard_map/ppermute | solution.py:22
  101.3 7.7 %collective-permute-start.3 = (f32[128,128]{0,1:T(8,128)S(1)}, f32[128,128]{0,1:T(8,128)S(1)}, u32[]{:S(2)}, u32[]{:S(2)}) collective-permute-start(f32[128,128]{0,1:T(8,128)S(1)} %maximum_select_fusion.4), channel_id=1, source_target_pairs={{0,2},{2,0},{1,3},{3,1},{4,6},{6,4},{5,7},{7,5},{8,10},{10,8},{9,1... | collective-permute-start | bytes 196616 | tf_op jit(solution)/shard_map/ppermute | solution.py:22
  111.1 2.3 copy-start.3
  111.4 96.4 %copy-start.9 = (bf16[128,256]{1,0:T(8,128)(2,1)S(1)}, bf16[128,256]{1,0:T(8,128)(2,1)}, u32[]{:S(2)}) copy-start(bf16[128,256]{1,0:T(8,128)(2,1)} %param.12) | copy-start | bytes 196612
  113.3 97.7 %copy-start.11 = (bf16[128,256]{1,0:T(8,128)(2,1)S(1)}, bf16[128,256]{1,0:T(8,128)(2,1)}, u32[]{:S(2)}) copy-start(bf16[128,256]{1,0:T(8,128)(2,1)} %param.13) | copy-start | bytes 196612
  113.4 165.4 %all-gather.5.cloned.1.call-start = ((), (), s32[]{:S(2)}) async-start(), calls=%async_computation.4 | async-start | bytes 2228224 | tf_op jit(solution)/shard_map/all_gather | solution.py:183
  208.7 3.0 copy-start.10
  208.7 2.3 collective-permute-start.4
  211.7 197.8 %reduce-scatter.5.cloned.1.call-start = ((), (), s32[]{:S(2)}) async-start(), calls=%async_computation.5 | async-start | bytes 2228224 | tf_op jit(solution)/shard_map/reduce_scatter | solution.py:185
  278.8 2.2 copy-start.2
  282.6 13.5 %copy-start.13 = (f32[64]{0:T(128)S(1)}, f32[64]{0:T(128)}, u32[]{:S(2)}) copy-start(f32[64]{0:T(128)} %copy-done.12) | copy-start | bytes 772
  282.6 5.8 %collective-permute-start.5 = (f32[128,64]{0,1:T(8,128)S(1)}, f32[128,64]{0,1:T(8,128)S(1)}, u32[]{:S(2)}, u32[]{:S(2)}) collective-permute-start(f32[128,64]{0,1:T(8,128)S(1)} %fusion.58), channel_id=1, source_target_pairs={{0,1},{1,0},{2,3},{3,2},{4,5},{5,4},{6,7},{7,6},{8,9},{9,8},{10,11... | collective-permute-start | bytes 98312 | tf_op jit(solution)/shard_map/ppermute | solution.py:22
  288.5 7.7 %collective-permute-start.6 = (f32[128,128]{0,1:T(8,128)S(1)}, f32[128,128]{0,1:T(8,128)S(1)}, u32[]{:S(2)}, u32[]{:S(2)}) collective-permute-start(f32[128,128]{0,1:T(8,128)S(1)} %maximum_select_fusion.5), channel_id=1, source_target_pairs={{0,2},{2,0},{1,3},{3,1},{4,6},{6,4},{5,7},{7,5},{8,10},{10,8},{9,1... | collective-permute-start | bytes 196616 | tf_op jit(solution)/shard_map/ppermute | solution.py:22
  302.2 107.3 %copy-start.7 = (f32[128,256]{1,0:T(8,128)S(1)}, f32[128,256]{1,0:T(8,128)}, u32[]{:S(2)}) copy-start(f32[128,256]{1,0:T(8,128)} %convert_select_fusion) | copy-start | bytes 393220
Sparse Core Ops, SparseCore 0:
  11.5 80.9 all-gather.2
  113.5 94.2 reduce-scatter.2
  211.8 66.9 all-gather.4
  304.3 105.1 reduce-scatter.4
where the time goes:
time: 416 us; the launch traced here: 418 us
  waiting for transfers between devices  345 us (83%)
  starting transfers between devices  26.9 us (6%)
  between operations  15 us (4%)
  matrix products  14.9 us (4%)
  other arithmetic  14.3 us (3%)
    reduce_scatter x2, waiting for transfers between devices, advance(): lax.psum_scatter(partial_out, 'head', scatter_dimension=1, tiled=True)  200 us
    all_gather x2, waiting for transfers between devices, advance(): full_rows = lax.all_gather(own_rows, 'head', axis=1, tiled=True)  129 us
    ppermute x6, starting transfers between devices, swapped(): return lax.ppermute(block, axis, route)  25.4 us
    ppermute x6, waiting for transfers between devices, swapped(): return lax.ppermute(block, axis, route)  16.1 us
  transfers between devices with their start and end apart: 11, of which 10 were waited for; matrix products, arithmetic and copies ran while one was open for 2% of the time, Pallas kernels for 0%

commit v1 on v0

v1 whole, which is shorter than its diff:
```python
import functools

import jax
import jax.numpy as jnp
from jax import lax
from jax.experimental import pallas as pl
from jax.experimental.pallas import tpu as pltpu
from jax.sharding import PartitionSpec as P

KVH = 4
HD = 128
EPSILON = 1e-05
ROPE_BASE = 1000000.0
NEGATIVE = -1e30
BLOCK = 1024
VMEM = pl.BlockSpec(memory_space=pltpu.VMEM)
SMEM = pl.BlockSpec(memory_space=pltpu.SMEM)
PARAMS = pltpu.CompilerParams(vmem_limit_bytes=24 * 1024 * 1024)


def rope_tables(positions):
    half = HD // 2
    exponent = jnp.arange(half, dtype=jnp.float32) * (2.0 / HD)
    inverse = jnp.power(jnp.float32(ROPE_BASE), -exponent)
    angles = positions[:, None] * inverse[None, :]
    cosine = jnp.cos(angles)
    sine = jnp.sin(angles)
    return (
        jnp.concatenate([cosine, cosine], axis=1),
        jnp.concatenate([-sine, sine], axis=1),
    )


def turned(entries, cosine, sine):
    return entries * cosine + pltpu.roll(entries, HD // 2, 1) * sine


def project_kernel(x_ref, gain_ref, wq_ref, wkv_ref, cos_ref, sin_ref, q_ref, kv_ref):
    chunks, rows, part = x_ref.shape
    squares = jnp.zeros((rows, part), jnp.float32)
    for c in range(chunks):
        piece = x_ref[c].astype(jnp.float32)
        squares = squares + piece * piece
    mean_square = jnp.sum(squares, axis=1, keepdims=True) / (chunks * part)
    inverse = lax.rsqrt(mean_square + EPSILON)
    queries = jnp.zeros((rows, HD), jnp.float32)
    keyval = jnp.zeros((rows, wkv_ref.shape[1]), jnp.float32)
    for c in range(chunks):
        piece = x_ref[c].astype(jnp.float32)
        normed = (piece * inverse * gain_ref[c]).astype(jnp.bfloat16)
        span = pl.ds(c * part, part)
        queries = queries + jnp.dot(normed, wq_ref[span, :], preferred_element_type=jnp.float32)
        keyval = keyval + jnp.dot(normed, wkv_ref[span, :], preferred_element_type=jnp.float32)
    q_ref[...] = turned(queries, cos_ref[...], sin_ref[...]).astype(jnp.bfloat16)
    flipped = keyval.T
    for peer in range(kv_ref.shape[0]):
        kv_ref[peer] = flipped


def attend_kernel(second, *refs):
    if second:
        (len_ref, q_ref, kv_ref, cos_ref, sin_ref, cache_ref, wout_ref, oldk_ref, oldv_ref, y_ref) = refs
    else:
        (len_ref, q_ref, kv_ref, cos_ref, sin_ref, cache_ref, wout_ref, y_ref, newk_ref, newv_ref) = refs
    rows = q_ref.shape[0]
    length = len_ref[0]
    scaling = HD ** (-0.5)
    queries = q_ref[...]
    keyval = kv_ref[...].T
    keys = turned(keyval[:, :HD], cos_ref[...], sin_ref[...]).astype(jnp.bfloat16)
    values = keyval[:, HD:].astype(jnp.bfloat16)
    row_ids = lax.broadcasted_iota(jnp.int32, (rows, rows), 0)
    key_ids = lax.broadcasted_iota(jnp.int32, (rows, rows), 1)

    def score(key_rows):
        return (
            lax.dot_general(
                queries, key_rows, (((1,), (1,)), ((), ())), preferred_element_type=jnp.float32
            )
            * scaling
        )

    def weigh(scores, value_rows, running):
        peak, total, out = running
        joined = jnp.maximum(peak, jnp.max(scores, axis=1, keepdims=True))
        shrink = jnp.exp(peak - joined)
        weights = jnp.exp(scores - joined)
        total = shrink * total + jnp.sum(weights, axis=1, keepdims=True)
        out = shrink * out + jnp.dot(
            weights.astype(jnp.bfloat16), value_rows, preferred_element_type=jnp.float32
        )
        return (joined, total, out)

    running = (
        jnp.full((rows, 1), NEGATIVE, jnp.float32),
        jnp.zeros((rows, 1), jnp.float32),
        jnp.zeros((rows, HD), jnp.float32),
    )
    running = weigh(jnp.where(key_ids <= row_ids, score(keys), NEGATIVE), values, running)
    if second:
        running = weigh(score(oldk_ref[...]), oldv_ref[...], running)
    else:
        newk_ref[...] = keys
        newv_ref[...] = values

    def whole_block(index, running):
        span = pl.ds(pl.multiple_of(index * BLOCK, BLOCK), BLOCK)
        return weigh(score(cache_ref[span, :HD]), cache_ref[span, HD:], running)

    def last_block(index, running):
        span = pl.ds(pl.multiple_of(index * BLOCK, BLOCK), BLOCK)
        places = index * BLOCK + lax.broadcasted_iota(jnp.int32, (rows, BLOCK), 1)
        scores = jnp.where(places < length, score(cache_ref[span, :HD]), NEGATIVE)
        return weigh(scores, cache_ref[span, HD:], running)

    full = length // BLOCK
    running = lax.fori_loop(0, full, whole_block, running)
    running = lax.fori_loop(full, (length + BLOCK - 1) // BLOCK, last_block, running)
    _, total, out = running
    attended = (out / total).astype(jnp.bfloat16)
    chunks, _, part = y_ref.shape
    for c in range(chunks):
        y_ref[c] = jnp.dot(
            attended, wout_ref[:, pl.ds(c * part, part)], preferred_element_type=jnp.float32
        ).astype(jnp.bfloat16)


def local(slices, new_slice, norm_gain, w_query, w_keyval, w_out, cached_rows, lengths):
    segment_index = lax.axis_index("segment")
    head_count = lax.axis_size("head")
    rows, part = slices.shape
    group = head_count // KVH
    groups = [[g * group + i for i in range(group)] for g in range(KVH)]
    key_columns = w_keyval.shape[2]
    cosines, sines = rope_tables(
        (lengths[0] + jnp.arange(2 * rows, dtype=jnp.int32)).astype(jnp.float32)
    )
    gain = norm_gain[0].reshape(head_count, 1, part)

    cache = lax.all_to_all(
        jnp.broadcast_to(cached_rows, (group,) + cached_rows.shape[1:]),
        "head", 0, 0, axis_index_groups=groups,
    ).reshape(group * cached_rows.shape[1], 2 * HD)

    def gathered(own):
        return lax.all_to_all(
            jnp.broadcast_to(own[None], (head_count, rows, part)), "head", 0, 0
        )

    def partial_outputs(own, turn, earlier):
        cos = cosines[turn * rows : (turn + 1) * rows]
        sin = sines[turn * rows : (turn + 1) * rows]
        queries, keyval = pl.pallas_call(
            project_kernel,
            out_shape=(
                jax.ShapeDtypeStruct((rows, HD), jnp.bfloat16),
                jax.ShapeDtypeStruct((group, key_columns, rows), jnp.float32),
            ),
            in_specs=[VMEM] * 6,
            out_specs=(VMEM, VMEM),
            compiler_params=PARAMS,
            name=f"project{turn}",
        )(gathered(own), gain, w_query[0], w_keyval[0], cos, sin)
        keyval = lax.all_to_all(keyval, "head", 0, 0, axis_index_groups=groups)
        keyval = keyval.reshape(group * key_columns, rows)
        outputs = [jax.ShapeDtypeStruct((head_count, rows, part), jnp.bfloat16)]
        if not earlier:
            outputs += [jax.ShapeDtypeStruct((rows, HD), jnp.bfloat16)] * 2
        results = pl.pallas_call(
            functools.partial(attend_kernel, bool(earlier)),
            out_shape=tuple(outputs),
            in_specs=[SMEM] + [VMEM] * (6 + len(earlier)),
            out_specs=tuple([VMEM] * len(outputs)),
            compiler_params=PARAMS,
            name=f"attend{turn}",
        )(lengths, queries, keyval, cos, sin, cache, w_out[0], *earlier)
        return results[0], tuple(results[1:])

    def reduced(partials):
        arrived = lax.all_to_all(partials, "head", 0, 0)
        return jnp.sum(arrived.astype(jnp.float32), axis=0)

    partials, recent = partial_outputs(slices, 0, ())
    first_out = slices.astype(jnp.float32) + reduced(partials)
    count = lax.axis_size("segment")
    arrived = lax.ppermute(first_out, "segment", [(i, i + 1) for i in range(count - 1)])
    entering = jnp.where(segment_index == 0, new_slice.astype(jnp.float32), arrived)
    partials, _ = partial_outputs(entering.astype(jnp.bfloat16), 1, recent)
    second_out = entering + reduced(partials)
    return (first_out, second_out)


def solution(mesh):
    placed = (
        P("segment", "head"),
        P(None, "head"),
        P("segment", None),
        P("segment", None, "head"),
        P("segment", None, "head"),
        P("segment", "head", None),
        P("segment", "head", None),
        P("segment"),
    )
    return jax.shard_map(
        local,
        mesh=mesh,
        in_specs=placed,
        out_specs=(P("segment", "head"), P("segment", "head")),
        check_vma=False,
    )
```

time: 416 us -> 145 us (0.35)
  the two profiles are of different devices: /device:TPU:2 before, /device:TPU:224 now
where the time goes in v1:
time: 145 us; the launch traced here: 144 us
  blocking collectives  101 us (70%)
  waiting for transfers between devices  19.3 us (13%)
  starting transfers between devices  9.07 us (6%)
  Pallas kernels  6.47 us (4%)
  local copies, waits for them, and re-layouts  3.7 us (3%)
  other arithmetic  2.33 us (2%)
    all_to_all x2, blocking collectives, reduced(): arrived = lax.all_to_all(partials, 'head', 0, 0)  37.1 us
    all_to_all x1, blocking collectives, local(): lax.all_to_all(jnp.broadcast_to(cached_rows, (group,) + cached_rows.shape...  26.9 us
    all_to_all x1, blocking collectives, gathered(): lax.all_to_all(jnp.broadcast_to(own[None], (head_count, rows, part)), 'he...  20.6 us
    all_to_all x2, blocking collectives, partial_outputs(): keyval = lax.all_to_all(keyval, 'head', 0, 0, axis_index_groups=groups)  16.7 us
    all_to_all x1, waiting for transfers between devices, gathered(): lax.all_to_all(jnp.broadcast_to(own[None], (head_count, rows, part)), 'he...  14.8 us
    all_to_all x1, starting transfers between devices, gathered(): lax.all_to_all(jnp.broadcast_to(own[None], (head_count, rows, part)), 'he...  7.17 us
    ppermute x1, waiting for transfers between devices, local(): lax.ppermute(first_out, 'segment', [(i, i + 1) for i in range(count - 1)])  4.55 us
    pallas_call x2, Pallas kernels, partial_outputs(): pl.pallas_call(functools.partial(attend_kernel, bool(earlier)), out_shape...  4.38 us
  transfers between devices with their start and end apart: 2, of which 2 were waited for; matrix products, arithmetic and copies ran while one was open for 2% of the time, Pallas kernels for 0%

profile of v1, /device:TPU:224, one launch (start us, length us, event | category | flops | bytes accessed | tf_op | source)
XLA Modules:
  0.0 143.7 jit_solution(7349476682305166085)
XLA Ops:
  0.6 1.9 %broadcast_in_dim.8 = bf16[16,128,256]{2,1,0:T(8,128)(2,1)} broadcast(bf16[128,256]{1,0:T(8,128)(2,1)} %param.8), dimensions={1,2} | broadcast | bytes 1114112 | tf_op jit(solution)/shard_map/broadcast_in_dim | solution.py:147
  2.6 7.2 %all-to-all-start = ((bf16[16,128,256]{2,1,0:T(8,128)(2,1)}), bf16[16,128,256]{2,1,0:T(8,128)(2,1)S(1)}, u32[]{:S(2)}, u32[]{:S(2)}) async-start(bf16[16,128,256]{2,1,0:T(8,128)(2,1)} %broadcast_in_dim.8), calls=%async_computation | async-start | bytes 2097152 | tf_op jit(solution)/shard_map/all_to_all | solution.py:146
  10.4 1.5 %copy.10 = bf16[1,4096,64]{2,1,0:T(8,128)(2,1)S(1)} copy(bf16[1,4096,64]{1,2,0:T(8,128)(2,1)} %param.12) | data formatting | bytes 1048576 | tf_op args[4]
  11.9 0.5 multiply_sine_fusion
  12.5 0.1 pad_maximum_fusion
  12.6 14.8 %all-to-all-done.x_ref = bf16[16,128,256]{2,1,0:T(8,128)(2,1)S(1)} async-done(((bf16[16,128,256]{2,1,0:T(8,128)(2,1)}), bf16[16,128,256]{2,1,0:T(8,128)(2,1)S(1)}, u32[]{:S(2)}, u32[]{:S(2)}) %all-to-all-start) | async-done | bytes 1048608 | tf_op jit(solution)/shard_map/all_to_all | solution.py:146
  27.4 0.0 copy-done
  27.4 0.0 copy-done.4
  27.4 1.0 project0.1
  28.5 8.4 %all_to_all.35 = f32[4,64,128]{2,1,0:T(8,128)S(1)} all-to-all(f32[4,64,128]{2,1,0:T(8,128)S(1)} %get-tuple-element.10), channel_id=1, replica_groups={{0,1,2,3},{4,5,6,7},{8,9,10,11},{12,13,14,15},{16,17,18,19},{20,21,22,2..., dimensions={0} | all-to-all | bytes 262144 | tf_op jit(solution)/shard_map/all_to_all | solution.py:164
  36.8 0.0 copy-done.5
  36.8 0.1 broadcast_in_dim.10
  37.0 0.0 copy-start.2
  37.0 26.9 %all_to_all.36 = bf16[4,1024,256]{2,1,0:T(8,128)(2,1)S(1)} all-to-all(bf16[4,1024,256]{2,1,0:T(8,128)(2,1)S(1)} %broadcast_in_dim.10), channel_id=1, replica_groups={{0,1,2,3},{4,5,6,7},{8,9,10,11},{12,13,14,15},{16,17,18,19},{20,21,22,2..., dimensions={0} | all-to-all | bytes 4194304 | tf_op jit(solution)/shard_map/all_to_all | solution.py:140
  63.9 2.1 %attend0.1 = (bf16[16,128,256]{2,1,0:T(8,128)(2,1)S(1)}, bf16[128,128]{1,0:T(8,128)(2,1)S(1)}, bf16[128,128]{1,0:T(8,128)(2,1)S(1)}) custom-call(s32[1]{0:T(128)} %copy.11.refs_0_, bf16[128,128]{1,0:T(8,128)(2,1)S(1)} %get-tuple-element.9.refs_1_, f32[256,128]{1,0:T(8,128)S(1)} %bitcast.18, f32[128,128]{1,0:T(8,128)S(1)} %get-tuple-element.23.cos_ref.refs_3_, ...), custom_call_target="tpu_custom_call" | custom-call | tf_op jit(solution)/shard_map/attend0/pallas_call | solution.py:169
  66.0 0.0 copy-start.6
  66.0 0.0 copy-start.7
  66.0 18.3 %all_to_all.37 = bf16[16,128,256]{2,1,0:T(8,128)(2,1)S(1)} all-to-all(bf16[16,128,256]{2,1,0:T(8,128)(2,1)S(1)} %get-tuple-element.11), channel_id=1, replica_groups=mesh['segment'=32,'head'=16] {'head'}, dimensions={0} | all-to-all | bytes 2097152 | tf_op jit(solution)/shard_map/all_to_all | solution.py:180
  84.3 0.1 convert_reduce_fusion.1
  84.4 0.7 convert_add_fusion
  85.1 1.9 %collective-permute-start = (f32[128,256]{1,0:T(8,128)}, f32[128,256]{1,0:T(8,128)S(1)}, u32[]{:S(2)}, u32[]{:S(2)}) collective-permute-start(f32[128,256]{1,0:T(8,128)} %convert_add_fusion), channel_id=1, source_target_pairs={{0,16},{16,32},{32,48},{48,64},{64,80},{80,96},{96,112},{112,128},... | collective-permute-start | bytes 393224 | tf_op jit(solution)/shard_map/ppermute | solution.py:186
  87.0 0.0 copy-start.1
  87.0 4.6 %collective-permute-done = f32[128,256]{1,0:T(8,128)S(1)} collective-permute-done((f32[128,256]{1,0:T(8,128)}, f32[128,256]{1,0:T(8,128)S(1)}, u32[]{:S(2)}, u32[]{:S(2)}) %collective-permute-start) | collective-permute-done | bytes 131104 | tf_op jit(solution)/shard_map/ppermute | solution.py:186
  91.6 0.1 broadcast_in_dim.11
  91.7 20.6 %all_to_all.38.x_ref = bf16[16,128,256]{2,1,0:T(8,128)(2,1)S(1)} all-to-all(bf16[16,128,256]{2,1,0:T(8,128)(2,1)S(1)} %broadcast_in_dim.11), channel_id=1, replica_groups=mesh['segment'=32,'head'=16] {'head'}, dimensions={0} | all-to-all | bytes 2097152 | tf_op jit(solution)/shard_map/all_to_all | solution.py:146
  112.3 0.0 copy-done.1
  112.3 1.0 project1.1
  113.4 8.4 %all_to_all.39 = f32[4,64,128]{2,1,0:T(8,128)S(1)} all-to-all(f32[4,64,128]{2,1,0:T(8,128)S(1)} %get-tuple-element.13), channel_id=1, replica_groups={{0,1,2,3},{4,5,6,7},{8,9,10,11},{12,13,14,15},{16,17,18,19},{20,21,22,2..., dimensions={0} | all-to-all | bytes 262144 | tf_op jit(solution)/shard_map/all_to_all | solution.py:164
  121.8 2.3 %attend1.1 = bf16[16,128,256]{2,1,0:T(8,128)(2,1)S(1)} custom-call(s32[1]{0:T(128)} %copy.11.refs_0_, bf16[128,128]{1,0:T(8,128)(2,1)S(1)} %get-tuple-element.12.refs_1_, f32[256,128]{1,0:T(8,128)S(1)} %bitcast.19, f32[128,128]{1,0:T(8,128)S(1)} %get-tuple-element.24.cos_ref.refs_3_, f32[128,128]{1,0:T(8,128)S(1)} %get-tuple-element.16.sin_ref.refs_4_, ...), custom_call_target="tpu_custom_call" | custom-call | tf_op jit(solution)/shard_map/attend1/pallas_call | solution.py:169
  124.1 18.8 %all_to_all.40 = bf16[16,128,256]{2,1,0:T(8,128)(2,1)S(1)} all-to-all(bf16[16,128,256]{2,1,0:T(8,128)(2,1)S(1)} %attend1.1), channel_id=1, replica_groups=mesh['segment'=32,'head'=16] {'head'}, dimensions={0} | all-to-all | bytes 2097152 | tf_op jit(solution)/shard_map/all_to_all | solution.py:180
  142.9 0.1 convert_reduce_fusion
  143.1 0.7 fusion
  (11 shorter events, 0.0 us)
Async XLA Ops:
  2.5 24.9 %copy-start = (bf16[1,4096,128]{2,1,0:T(8,128)(2,1)S(1)}, bf16[1,4096,128]{2,1,0:T(8,128)(2,1)}, u32[]{:S(2)}) copy-start(bf16[1,4096,128]{2,1,0:T(8,128)(2,1)} %param.11) | copy-start | bytes 3145732
  2.5 24.9 %copy-start.4 = (f32[1,4096]{1,0:T(1,128)S(1)}, f32[1,4096]{1,0:T(1,128)}, u32[]{:S(2)}) copy-start(f32[1,4096]{1,0:T(1,128)} %param.10) | copy-start | bytes 49156
  2.6 24.8 %all-to-all-start = ((bf16[16,128,256]{2,1,0:T(8,128)(2,1)}), bf16[16,128,256]{2,1,0:T(8,128)(2,1)S(1)}, u32[]{:S(2)}, u32[]{:S(2)}) async-start(bf16[16,128,256]{2,1,0:T(8,128)(2,1)} %broadcast_in_dim.8), calls=%async_computation | async-start | bytes 2097152 | tf_op jit(solution)/shard_map/all_to_all | solution.py:146
  27.4 9.4 %copy-start.5 = (bf16[1,1024,256]{2,1,0:T(8,128)(2,1)S(1)}, bf16[1,1024,256]{2,1,0:T(8,128)(2,1)}, u32[]{:S(2)}) copy-start(bf16[1,1024,256]{2,1,0:T(8,128)(2,1)} %param.14) | copy-start | bytes 1572868
  37.0 27.0 %copy-start.2 = (bf16[1,128,4096]{2,1,0:T(8,128)(2,1)S(1)}, bf16[1,128,4096]{2,1,0:T(8,128)(2,1)}, u32[]{:S(2)}) copy-start(bf16[1,128,4096]{2,1,0:T(8,128)(2,1)} %param.13) | copy-start | bytes 3145732
  66.0 18.4 %copy-start.6 = (bf16[128,256]{1,0:T(8,128)(2,1)S(1)}, bf16[128,256]{1,0:T(8,128)(2,1)}, u32[]{:S(2)}) copy-start(bf16[128,256]{1,0:T(8,128)(2,1)} %param.8) | copy-start | bytes 196612
  66.0 25.6 %copy-start.7 = (bf16[128,256]{1,0:T(8,128)(2,1)S(1)}, bf16[128,256]{1,0:T(8,128)(2,1)}, u32[]{:S(2)}) copy-start(bf16[128,256]{1,0:T(8,128)(2,1)} %param.9) | copy-start | bytes 196612
  85.1 6.5 %collective-permute-start = (f32[128,256]{1,0:T(8,128)}, f32[128,256]{1,0:T(8,128)S(1)}, u32[]{:S(2)}, u32[]{:S(2)}) collective-permute-start(f32[128,256]{1,0:T(8,128)} %convert_add_fusion), channel_id=1, source_target_pairs={{0,16},{16,32},{32,48},{48,64},{64,80},{80,96},{96,112},{112,128},... | collective-permute-start | bytes 393224 | tf_op jit(solution)/shard_map/ppermute | solution.py:186
  87.0 25.3 %copy-start.1 = (bf16[1,4096,128]{2,1,0:T(8,128)(2,1)S(1)}, bf16[1,4096,128]{2,1,0:T(8,128)(2,1)}, u32[]{:S(2)}) copy-start(bf16[1,4096,128]{2,1,0:T(8,128)(2,1)} %param.11) | copy-start | bytes 3145732
  112.3 9.4 %copy-start.3 = (bf16[1,128,4096]{2,1,0:T(8,128)(2,1)S(1)}, bf16[1,128,4096]{2,1,0:T(8,128)(2,1)}, u32[]{:S(2)}) copy-start(bf16[1,128,4096]{2,1,0:T(8,128)(2,1)} %param.13) | copy-start | bytes 3145732

commit v2 on v1

v2 whole, which is shorter than its diff:
```python
import functools

import jax
import jax.numpy as jnp
from jax import lax
from jax.experimental import pallas as pl
from jax.experimental.pallas import tpu as pltpu
from jax.sharding import PartitionSpec as P

KVH = 4
HD = 128
EPSILON = 1e-05
ROPE_BASE = 1000000.0
NEGATIVE = -1e30
VMEM = pl.BlockSpec(memory_space=pltpu.VMEM)
SMEM = pl.BlockSpec(memory_space=pltpu.SMEM)
PARAMS = pltpu.CompilerParams(vmem_limit_bytes=24 * 1024 * 1024)


def rope_tables(positions):
    half = HD // 2
    exponent = jnp.arange(half, dtype=jnp.float32) * (2.0 / HD)
    inverse = jnp.power(jnp.float32(ROPE_BASE), -exponent)
    angles = positions[:, None] * inverse[None, :]
    cosine = jnp.cos(angles)
    sine = jnp.sin(angles)
    return (
        jnp.concatenate([cosine, cosine], axis=1),
        jnp.concatenate([-sine, sine], axis=1),
    )


def turned(entries, cosine, sine):
    return entries * cosine + pltpu.roll(entries, HD // 2, 1) * sine


def project_kernel(place_ref, x_ref, gain_ref, wq_ref, wkv_ref, cos_ref, sin_ref, packed_ref):
    chunks, rows, part = x_ref.shape
    squares = jnp.zeros((rows, part), jnp.float32)
    for c in range(chunks):
        piece = x_ref[c].astype(jnp.float32)
        squares = squares + piece * piece
    mean_square = jnp.sum(squares, axis=1, keepdims=True) / (chunks * part)
    inverse = lax.rsqrt(mean_square + EPSILON)
    queries = jnp.zeros((rows, HD), jnp.float32)
    keyval = jnp.zeros((rows, wkv_ref.shape[0]), jnp.float32)
    for c in range(chunks):
        piece = x_ref[c].astype(jnp.float32)
        normed = (piece * inverse * gain_ref[c]).astype(jnp.bfloat16)
        span = pl.ds(c * part, part)
        queries = queries + jnp.dot(normed, wq_ref[span, :], preferred_element_type=jnp.float32)
        keyval = keyval + lax.dot_general(
            normed, wkv_ref[:, span], (((1,), (1,)), ((), ())), preferred_element_type=jnp.float32
        )
    queries = turned(queries, cos_ref[...], sin_ref[...]).astype(jnp.bfloat16)
    flipped = keyval.T
    high = flipped.astype(jnp.bfloat16)
    low = (flipped - high.astype(jnp.float32)).astype(jnp.bfloat16)
    columns = flipped.shape[0]
    for peer in range(packed_ref.shape[0]):
        packed_ref[peer, pl.ds(0, rows)] = queries
        packed_ref[peer, pl.ds(rows, columns)] = high
        packed_ref[peer, pl.ds(rows + columns, columns)] = low


def score(queries, key_rows):
    return lax.dot_general(
        queries, key_rows, (((1,), (1,)), ((), ())), preferred_element_type=jnp.float32
    ) * HD ** (-0.5)


def cached_kernel(place_ref, packed_ref, cache_ref, partial_ref):
    group = packed_ref.shape[0]
    rows = partial_ref.shape[1] - 8
    span = cache_ref.shape[0]
    live = place_ref[0] - place_ref[1] * span
    places = lax.broadcasted_iota(jnp.int32, (1, span), 1)
    hidden = jnp.where(places < live, 0.0, NEGATIVE)
    queries = packed_ref[:, pl.ds(0, rows), :].reshape(group * rows, HD)
    scores = score(queries, cache_ref[:, :HD]) + hidden
    peak = jnp.max(scores, axis=1, keepdims=True)
    weights = jnp.exp(scores - peak)
    total = jnp.sum(weights, axis=1, keepdims=True)
    out = jnp.dot(
        weights.astype(jnp.bfloat16), cache_ref[:, HD:], preferred_element_type=jnp.float32
    )
    for head in range(group):
        at = slice(head * rows, (head + 1) * rows)
        partial_ref[head, pl.ds(0, rows)] = out[at]
        peaks = jnp.broadcast_to(peak[at], (rows, HD)).T
        totals = jnp.broadcast_to(total[at], (rows, HD)).T
        partial_ref[head, pl.ds(rows, 4)] = peaks[:4]
        partial_ref[head, pl.ds(rows + 4, 4)] = totals[:4]


def finish_kernel(second, *refs):
    (place_ref, packed_ref, cos_ref, sin_ref, partial_ref, wout_ref) = refs[:6]
    if second:
        (old_ref, y_ref) = refs[6:]
    else:
        (y_ref, new_ref) = refs[6:]
    group = packed_ref.shape[0]
    rows = partial_ref.shape[1] - 8
    columns = (packed_ref.shape[1] - rows) // 2
    queries = packed_ref[place_ref[1], pl.ds(0, rows), :]
    keyval = jnp.concatenate(
        [
            packed_ref[peer, pl.ds(rows, columns), :].astype(jnp.float32)
            + packed_ref[peer, pl.ds(rows + columns, columns), :].astype(jnp.float32)
            for peer in range(group)
        ],
        axis=0,
    ).T
    keys = turned(keyval[:, :HD], cos_ref[...], sin_ref[...]).astype(jnp.bfloat16)
    values = keyval[:, HD:].astype(jnp.bfloat16)
    row_ids = lax.broadcasted_iota(jnp.int32, (rows, rows), 0)
    key_ids = lax.broadcasted_iota(jnp.int32, (rows, rows), 1)
    fresh = [(jnp.where(key_ids <= row_ids, score(queries, keys), NEGATIVE), values)]
    if second:
        fresh.append((score(queries, old_ref[0]), old_ref[1]))
    else:
        new_ref[0] = keys
        new_ref[1] = values
    peaks = fresh[0][0]
    for scores, _ in fresh[1:]:
        peaks = jnp.maximum(peaks, scores)
    peak = jnp.broadcast_to(jnp.max(peaks, axis=1, keepdims=True), (rows, HD))
    stats = []
    for peer in range(group):
        part_peak = jnp.broadcast_to(partial_ref[peer, pl.ds(rows, 1)], (HD, rows)).T
        part_total = jnp.broadcast_to(partial_ref[peer, pl.ds(rows + 4, 1)], (HD, rows)).T
        peak = jnp.maximum(peak, part_peak)
        stats.append((part_peak, part_total))
    total = jnp.zeros((rows, HD), jnp.float32)
    out = jnp.zeros((rows, HD), jnp.float32)
    for scores, value_rows in fresh:
        weights = jnp.exp(scores - peak)
        total = total + jnp.sum(weights, axis=1, keepdims=True)
        out = out + jnp.dot(
            weights.astype(jnp.bfloat16), value_rows, preferred_element_type=jnp.float32
        )
    for peer, (part_peak, part_total) in enumerate(stats):
        shrink = jnp.exp(part_peak - peak)
        total = total + shrink * part_total
        out = out + shrink * partial_ref[peer, pl.ds(0, rows)]
    attended = (out / total).astype(jnp.bfloat16)
    chunks, _, part = y_ref.shape
    for c in range(chunks):
        y_ref[c] = jnp.dot(
            attended, wout_ref[:, pl.ds(c * part, part)], preferred_element_type=jnp.float32
        ).astype(jnp.bfloat16)


def local(slices, new_slice, norm_gain, w_query, w_keyval, w_out, cached_rows, lengths):
    segment_index = lax.axis_index("segment")
    head_count = lax.axis_size("head")
    rows, part = slices.shape
    group = head_count // KVH
    groups = [[g * group + i for i in range(group)] for g in range(KVH)]
    key_columns = w_keyval.shape[2]
    cosines, sines = rope_tables(
        (lengths[0] + jnp.arange(2 * rows, dtype=jnp.int32)).astype(jnp.float32)
    )
    gain = norm_gain[0].reshape(head_count, 1, part)

    place = jnp.stack([lengths[0], lax.axis_index("head") % group])
    keyval_weights = w_keyval[0].T

    def gathered(own):
        return lax.all_to_all(
            jnp.broadcast_to(own[None], (head_count, rows, part)), "head", 0, 0
        )

    def partial_outputs(everything, turn, earlier):
        cos = cosines[turn * rows : (turn + 1) * rows]
        sin = sines[turn * rows : (turn + 1) * rows]
        packed = pl.pallas_call(
            project_kernel,
            out_shape=jax.ShapeDtypeStruct((group, rows + 2 * key_columns, HD), jnp.bfloat16),
            in_specs=[SMEM] + [VMEM] * 6,
            out_specs=VMEM,
            compiler_params=PARAMS,
            name=f"project{turn}",
        )(place, everything, gain, w_query[0], keyval_weights, cos, sin)
        packed = lax.all_to_all(packed, "head", 0, 0, axis_index_groups=groups)
        partial = pl.pallas_call(
            cached_kernel,
            out_shape=jax.ShapeDtypeStruct((group, rows + 8, HD), jnp.float32),
            in_specs=[SMEM, VMEM, VMEM],
            out_specs=VMEM,
            compiler_params=PARAMS,
            name=f"cached{turn}",
        )(place, packed, cached_rows[0])
        partial = lax.all_to_all(partial, "head", 0, 0, axis_index_groups=groups)
        outputs = [jax.ShapeDtypeStruct((head_count, rows, part), jnp.bfloat16)]
        if not earlier:
            outputs += [jax.ShapeDtypeStruct((2, rows, HD), jnp.bfloat16)]
        results = pl.pallas_call(
            functools.partial(finish_kernel, bool(earlier)),
            out_shape=tuple(outputs),
            in_specs=[SMEM] + [VMEM] * (5 + len(earlier)),
            out_specs=tuple([VMEM] * len(outputs)),
            compiler_params=PARAMS,
            name=f"finish{turn}",
        )(place, packed, cos, sin, partial, w_out[0], *earlier)
        return results[0], tuple(results[1:])

    def reduced(partials):
        arrived = lax.all_to_all(partials, "head", 0, 0)
        return jnp.sum(arrived.astype(jnp.float32), axis=0)

    partials, recent = partial_outputs(gathered(slices), 0, ())
    first_out = slices.astype(jnp.float32) + reduced(partials)
    count = lax.axis_size("segment")
    route = [(i, i + 1) for i in range(count - 1)]
    arrived = lax.ppermute(first_out.astype(jnp.bfloat16), "segment", route)
    entering = jnp.where(segment_index == 0, new_slice, arrived)
    partials, _ = partial_outputs(gathered(entering), 1, recent)
    second_out = entering.astype(jnp.float32) + reduced(partials)
    return (first_out, second_out)


def solution(mesh):
    placed = (
        P("segment", "head"),
        P(None, "head"),
        P("segment", None),
        P("segment", None, "head"),
        P("segment", None, "head"),
        P("segment", "head", None),
        P("segment", "head", None),
        P("segment"),
    )
    return jax.shard_map(
        local,
        mesh=mesh,
        in_specs=placed,
        out_specs=(P("segment", "head"), P("segment", "head")),
        check_vma=False,
    )
```

time: 145 us -> 140 us (0.966)
  the two profiles are of different devices: /device:TPU:224 before, /device:TPU:96 now
where the time goes in v2:
time: 140 us; the launch traced here: 139 us
  blocking collectives  93.1 us (66%)
  waiting for transfers between devices  20 us (14%)
  Pallas kernels  10.1 us (7%)
  starting transfers between devices  9.07 us (6%)
  local copies, waits for them, and re-layouts  2.73 us (2%)
  other arithmetic  2.41 us (2%)
  between operations  1.52 us (1%)
    all_to_all x2, blocking collectives, reduced(): arrived = lax.all_to_all(partials, 'head', 0, 0)  34.8 us
    all_to_all x1, blocking collectives, gathered(): lax.all_to_all(jnp.broadcast_to(own[None], (head_count, rows, part)), 'he...  21.5 us
    all_to_all x2, blocking collectives, partial_outputs(): packed = lax.all_to_all(packed, 'head', 0, 0, axis_index_groups=groups)  18.6 us
    all_to_all x2, blocking collectives, partial_outputs(): partial = lax.all_to_all(partial, 'head', 0, 0, axis_index_groups=groups)  18.2 us
    all_to_all x1, waiting for transfers between devices, gathered(): lax.all_to_all(jnp.broadcast_to(own[None], (head_count, rows, part)), 'he...  16.1 us
    all_to_all x1, starting transfers between devices, gathered(): lax.all_to_all(jnp.broadcast_to(own[None], (head_count, rows, part)), 'he...  7.17 us
    pallas_call x2, Pallas kernels, partial_outputs(): pl.pallas_call(cached_kernel, out_shape=jax.ShapeDtypeStruct((group, rows...  3.88 us
    ppermute x1, waiting for transfers between devices, local(): arrived = lax.ppermute(first_out.astype(jnp.bfloat16), 'segment', route)  3.86 us
  transfers between devices with their start and end apart: 2, of which 2 were waited for; matrix products, arithmetic and copies ran while one was open for 1% of the time, Pallas kernels for 0%

profile of v2, /device:TPU:96, one launch (start us, length us, event | category | flops | bytes accessed | tf_op | source)
XLA Modules:
  0.0 139.0 jit_solution(5750813509672041313)
XLA Ops:
  0.6 1.9 %broadcast_in_dim.4 = bf16[16,128,256]{2,1,0:T(8,128)(2,1)} broadcast(bf16[128,256]{1,0:T(8,128)(2,1)} %param.8), dimensions={1,2} | broadcast | bytes 1114112 | tf_op jit(solution)/shard_map/broadcast_in_dim | solution.py:171
  2.5 7.2 %all-to-all-start = ((bf16[16,128,256]{2,1,0:T(8,128)(2,1)}), bf16[16,128,256]{2,1,0:T(8,128)(2,1)S(1)}, u32[]{:S(2)}, u32[]{:S(2)}) async-start(bf16[16,128,256]{2,1,0:T(8,128)(2,1)} %broadcast_in_dim.4), calls=%async_computation | async-start | bytes 2097152 | tf_op jit(solution)/shard_map/all_to_all | solution.py:170
  9.7 0.0 copy-start
  9.7 0.0 copy-start.4
  10.5 0.1 pad_add_fusion.place_ref.refs_0_
  10.6 0.5 multiply_sine_fusion
  11.1 0.1 pad_maximum_fusion
  11.3 16.1 %all-to-all-done.x_ref = bf16[16,128,256]{2,1,0:T(8,128)(2,1)S(1)} async-done(((bf16[16,128,256]{2,1,0:T(8,128)(2,1)}), bf16[16,128,256]{2,1,0:T(8,128)(2,1)S(1)}, u32[]{:S(2)}, u32[]{:S(2)}) %all-to-all-start) | async-done | bytes 1048608 | tf_op jit(solution)/shard_map/all_to_all | solution.py:170
  27.4 0.0 copy-done.2
  27.4 0.0 copy-start.3
  27.4 1.6 %project0.1 = bf16[4,256,128]{2,1,0:T(8,128)(2,1)S(1)} custom-call(s32[2]{0:T(128)S(1)} %pad_add_fusion.place_ref.refs_0_, bf16[16,128,256]{2,1,0:T(8,128)(2,1)S(1)} %all-to-all-done.x_ref, f32[16,1,256]{2,1,0:T(1,128)S(1)} %bitcast.18, bf16[4096,128]{1,0:T(8,128)(2,1)S(1)} %bitcast.10, bf16[64,4096]{1,0:T(8,128)(2,1)S(1)} %bitcast.14, ...), custom_call_target="tpu_custom_call" | custom-call | tf_op jit(solution)/shard_map/project0/pallas_call | solution.py:177
  29.0 0.0 copy-start.1
  29.0 9.2 %all_to_all.40.packed_ref.refs_1_ = bf16[4,256,128]{2,1,0:T(8,128)(2,1)S(1)} all-to-all(bf16[4,256,128]{2,1,0:T(8,128)(2,1)S(1)} %project0.1), channel_id=1, replica_groups={{0,1,2,3},{4,5,6,7},{8,9,10,11},{12,13,14,15},{16,17,18,19},{20,21,22,2..., dimensions={0} | all-to-all | bytes 524288 | tf_op jit(solution)/shard_map/all_to_all | solution.py:185
  38.2 1.9 %cached0.1 = f32[4,136,128]{2,1,0:T(8,128)S(1)} custom-call(s32[2]{0:T(128)S(1)} %pad_add_fusion.place_ref.refs_0_, bf16[4,256,128]{2,1,0:T(8,128)(2,1)S(1)} %all_to_all.40.packed_ref.refs_1_, bf16[1024,256]{1,0:T(8,128)(2,1)S(1)} %bitcast.16), custom_call_target="tpu_custom_call" | custom-call | tf_op jit(solution)/shard_map/cached0/pallas_call | solution.py:186
  40.2 9.1 %all_to_all.41.refs_4_ = f32[4,136,128]{2,1,0:T(8,128)S(1)} all-to-all(f32[4,136,128]{2,1,0:T(8,128)S(1)} %cached0.1), channel_id=1, replica_groups={{0,1,2,3},{4,5,6,7},{8,9,10,11},{12,13,14,15},{16,17,18,19},{20,21,22,2..., dimensions={0} | all-to-all | bytes 557056 | tf_op jit(solution)/shard_map/all_to_all | solution.py:194
  49.3 1.5 %finish0.1 = (bf16[16,128,256]{2,1,0:T(8,128)(2,1)S(1)}, bf16[2,128,128]{2,1,0:T(8,128)(2,1)S(1)}) custom-call(s32[2]{0:T(128)S(1)} %pad_add_fusion.place_ref.refs_0_, bf16[4,256,128]{2,1,0:T(8,128)(2,1)S(1)} %all_to_all.40.packed_ref.refs_1_, f32[128,128]{1,0:T(8,128)S(1)} %get-tuple-element.15.cos_ref.refs_2_, ...), custom_call_target="tpu_custom_call" | custom-call | tf_op jit(solution)/shard_map/finish0/pallas_call | solution.py:198
  50.8 16.9 %all_to_all.42 = bf16[16,128,256]{2,1,0:T(8,128)(2,1)S(1)} all-to-all(bf16[16,128,256]{2,1,0:T(8,128)(2,1)S(1)} %get-tuple-element.4), channel_id=1, replica_groups=mesh['segment'=32,'head'=16] {'head'}, dimensions={0} | all-to-all | bytes 2097152 | tf_op jit(solution)/shard_map/all_to_all | solution.py:209
  67.7 0.1 convert_reduce_fusion.1
  67.8 0.7 copy-done.5
  68.5 0.7 fusion.3
  69.2 1.9 %collective-permute-start = (bf16[128,256]{1,0:T(8,128)(2,1)}, bf16[128,256]{1,0:T(8,128)(2,1)S(1)}, u32[]{:S(2)}, u32[]{:S(2)}) collective-permute-start(bf16[128,256]{1,0:T(8,128)(2,1)} %get-tuple-element.6), channel_id=1, source_target_pairs={{0,16},{16,32},{32,48},{48,64},{64,80},{80,96},{96,112},{112,128},... | collective-permute-start | bytes 196616 | tf_op jit(solution)/shard_map/ppermute | solution.py:216
  71.1 3.9 %collective-permute-done = bf16[128,256]{1,0:T(8,128)(2,1)S(1)} collective-permute-done((bf16[128,256]{1,0:T(8,128)(2,1)}, bf16[128,256]{1,0:T(8,128)(2,1)S(1)}, u32[]{:S(2)}, u32[]{:S(2)}) %collective-permute-start) | collective-permute-done | bytes 65568 | tf_op jit(solution)/shard_map/ppermute | solution.py:216
  75.0 0.1 broadcast_in_dim.5
  75.1 21.5 %all_to_all.43.x_ref = bf16[16,128,256]{2,1,0:T(8,128)(2,1)S(1)} all-to-all(bf16[16,128,256]{2,1,0:T(8,128)(2,1)S(1)} %broadcast_in_dim.5), channel_id=1, replica_groups=mesh['segment'=32,'head'=16] {'head'}, dimensions={0} | all-to-all | bytes 2097152 | tf_op jit(solution)/shard_map/all_to_all | solution.py:170
  96.7 1.6 %project1.1 = bf16[4,256,128]{2,1,0:T(8,128)(2,1)S(1)} custom-call(s32[2]{0:T(128)S(1)} %pad_add_fusion.place_ref.refs_0_, bf16[16,128,256]{2,1,0:T(8,128)(2,1)S(1)} %all_to_all.43.x_ref, f32[16,1,256]{2,1,0:T(1,128)S(1)} %bitcast.19, bf16[4096,128]{1,0:T(8,128)(2,1)S(1)} %bitcast.11, bf16[64,4096]{1,0:T(8,128)(2,1)S(1)} %bitcast.15, ...), custom_call_target="tpu_custom_call" | custom-call | tf_op jit(solution)/shard_map/project1/pallas_call | solution.py:177
  98.3 9.4 %all_to_all.44.packed_ref.refs_1_ = bf16[4,256,128]{2,1,0:T(8,128)(2,1)S(1)} all-to-all(bf16[4,256,128]{2,1,0:T(8,128)(2,1)S(1)} %project1.1), channel_id=1, replica_groups={{0,1,2,3},{4,5,6,7},{8,9,10,11},{12,13,14,15},{16,17,18,19},{20,21,22,2..., dimensions={0} | all-to-all | bytes 524288 | tf_op jit(solution)/shard_map/all_to_all | solution.py:185
  107.6 1.9 %cached1.1 = f32[4,136,128]{2,1,0:T(8,128)S(1)} custom-call(s32[2]{0:T(128)S(1)} %pad_add_fusion.place_ref.refs_0_, bf16[4,256,128]{2,1,0:T(8,128)(2,1)S(1)} %all_to_all.44.packed_ref.refs_1_, bf16[1024,256]{1,0:T(8,128)(2,1)S(1)} %bitcast.17), custom_call_target="tpu_custom_call" | custom-call | tf_op jit(solution)/shard_map/cached1/pallas_call | solution.py:186
  109.6 9.1 %all_to_all.45.refs_4_ = f32[4,136,128]{2,1,0:T(8,128)S(1)} all-to-all(f32[4,136,128]{2,1,0:T(8,128)S(1)} %cached1.1), channel_id=1, replica_groups={{0,1,2,3},{4,5,6,7},{8,9,10,11},{12,13,14,15},{16,17,18,19},{20,21,22,2..., dimensions={0} | all-to-all | bytes 557056 | tf_op jit(solution)/shard_map/all_to_all | solution.py:194
  118.7 1.5 %finish1.1 = bf16[16,128,256]{2,1,0:T(8,128)(2,1)S(1)} custom-call(s32[2]{0:T(128)S(1)} %pad_add_fusion.place_ref.refs_0_, bf16[4,256,128]{2,1,0:T(8,128)(2,1)S(1)} %all_to_all.44.packed_ref.refs_1_, f32[128,128]{1,0:T(8,128)S(1)} %get-tuple-element.16.cos_ref.refs_2_, f32[128,128]{1,0:T(8,128)S(1)} %get-tuple-element.8.sin_ref.refs_3_, ...), custom_call_target="tpu_custom_call" | custom-call | tf_op jit(solution)/shard_map/finish1/pallas_call | solution.py:198
  120.3 17.9 %all_to_all.46 = bf16[16,128,256]{2,1,0:T(8,128)(2,1)S(1)} all-to-all(bf16[16,128,256]{2,1,0:T(8,128)(2,1)S(1)} %finish1.1), channel_id=1, replica_groups=mesh['segment'=32,'head'=16] {'head'}, dimensions={0} | all-to-all | bytes 2097152 | tf_op jit(solution)/shard_map/all_to_all | solution.py:209
  138.2 0.1 convert_reduce_fusion
  138.3 0.7 convert_add_fusion
  (11 shorter events, 0.0 us)
Async XLA Ops:
  2.5 24.9 %copy-start.2 = (bf16[1,4096,64]{1,2,0:T(8,128)(2,1)S(1)}, bf16[1,4096,64]{1,2,0:T(8,128)(2,1)}, u32[]{:S(2)}) copy-start(bf16[1,4096,64]{1,2,0:T(8,128)(2,1)} %param.12) | copy-start | bytes 1572868
  2.5 24.8 %all-to-all-start = ((bf16[16,128,256]{2,1,0:T(8,128)(2,1)}), bf16[16,128,256]{2,1,0:T(8,128)(2,1)S(1)}, u32[]{:S(2)}, u32[]{:S(2)}) async-start(bf16[16,128,256]{2,1,0:T(8,128)(2,1)} %broadcast_in_dim.4), calls=%async_computation | async-start | bytes 2097152 | tf_op jit(solution)/shard_map/all_to_all | solution.py:170
  9.7 17.7 %copy-start = (bf16[1,4096,128]{2,1,0:T(8,128)(2,1)S(1)}, bf16[1,4096,128]{2,1,0:T(8,128)(2,1)}, u32[]{:S(2)}) copy-start(bf16[1,4096,128]{2,1,0:T(8,128)(2,1)} %param.11) | copy-start | bytes 3145732
  9.7 17.7 %copy-start.4 = (f32[1,4096]{1,0:T(1,128)S(1)}, f32[1,4096]{1,0:T(1,128)}, u32[]{:S(2)}) copy-start(f32[1,4096]{1,0:T(1,128)} %param.10) | copy-start | bytes 49156
  27.4 10.8 %copy-start.3 = (bf16[1,1024,256]{2,1,0:T(8,128)(2,1)S(1)}, bf16[1,1024,256]{2,1,0:T(8,128)(2,1)}, u32[]{:S(2)}) copy-start(bf16[1,1024,256]{2,1,0:T(8,128)(2,1)} %param.14) | copy-start | bytes 1572868
  29.0 20.3 %copy-start.1 = (bf16[1,128,4096]{2,1,0:T(8,128)(2,1)S(1)}, bf16[1,128,4096]{2,1,0:T(8,128)(2,1)}, u32[]{:S(2)}) copy-start(bf16[1,128,4096]{2,1,0:T(8,128)(2,1)} %param.13) | copy-start | bytes 3145732
  67.7 0.8 copy-start.5
  67.7 7.3 %copy-start.6 = (bf16[128,256]{1,0:T(8,128)(2,1)S(1)}, bf16[128,256]{1,0:T(8,128)(2,1)}, u32[]{:S(2)}) copy-start(bf16[128,256]{1,0:T(8,128)(2,1)} %param.9) | copy-start | bytes 196612
  69.2 5.8 %collective-permute-start = (bf16[128,256]{1,0:T(8,128)(2,1)}, bf16[128,256]{1,0:T(8,128)(2,1)S(1)}, u32[]{:S(2)}, u32[]{:S(2)}) collective-permute-start(bf16[128,256]{1,0:T(8,128)(2,1)} %get-tuple-element.6), channel_id=1, source_target_pairs={{0,16},{16,32},{32,48},{48,64},{64,80},{80,96},{96,112},{112,128},... | collective-permute-start | bytes 196616 | tf_op jit(solution)/shard_map/ppermute | solution.py:216

commit v3 on v2

--- a/solution.py
+++ b/solution.py
@@ -22,19 +22,21 @@
     exponent = jnp.arange(half, dtype=jnp.float32) * (2.0 / HD)
     inverse = jnp.power(jnp.float32(ROPE_BASE), -exponent)
     angles = positions[:, None] * inverse[None, :]
-    cosine = jnp.cos(angles)
-    sine = jnp.sin(angles)
-    return (
-        jnp.concatenate([cosine, cosine], axis=1),
-        jnp.concatenate([-sine, sine], axis=1),
-    )
-
-
-def turned(entries, cosine, sine):
-    return entries * cosine + pltpu.roll(entries, HD // 2, 1) * sine
-
-
-def project_kernel(place_ref, x_ref, gain_ref, wq_ref, wkv_ref, cos_ref, sin_ref, packed_ref):
+    return jnp.cos(angles), jnp.sin(angles)
+
+
+def turned(entries, cos_ref, sin_ref, turn):
+    span = pl.ds(turn * entries.shape[0], entries.shape[0])
+    cosine = cos_ref[span, :]
+    sine = sin_ref[span, :]
+    return entries * jnp.concatenate([cosine, cosine], axis=1) + pltpu.roll(
+        entries, HD // 2, 1
+    ) * jnp.concatenate([-sine, sine], axis=1)
+
+
+def project_kernel(
+    turn, place_ref, x_ref, gain_ref, wq_ref, wkv_ref, cos_ref, sin_ref, packed_ref, own_ref
+):
     chunks, rows, part = x_ref.shape
     squares = jnp.zeros((rows, part), jnp.float32)
     for c in range(chunks):
@@ -52,15 +54,12 @@
         keyval = keyval + lax.dot_general(
             normed, wkv_ref[:, span], (((1,), (1,)), ((), ())), preferred_element_type=jnp.float32
         )
-    queries = turned(queries, cos_ref[...], sin_ref[...]).astype(jnp.bfloat16)
-    flipped = keyval.T
-    high = flipped.astype(jnp.bfloat16)
-    low = (flipped - high.astype(jnp.float32)).astype(jnp.bfloat16)
-    columns = flipped.shape[0]
+    queries = turned(queries, cos_ref, sin_ref, turn).astype(jnp.bfloat16)
+    flipped = keyval.T.astype(jnp.bfloat16)
     for peer in range(packed_ref.shape[0]):
         packed_ref[peer, pl.ds(0, rows)] = queries
-        packed_ref[peer, pl.ds(rows, columns)] = high
-        packed_ref[peer, pl.ds(rows + columns, columns)] = low
+        packed_ref[peer, pl.ds(rows, flipped.shape[0])] = flipped
+    own_ref[...] = x_ref[place_ref[2]]
 
 
 def score(queries, key_rows):
@@ -69,9 +68,18 @@
     ) * HD ** (-0.5)
 
 
+def thirds(value):
+    pieces = []
+    for _ in range(3):
+        piece = value.astype(jnp.bfloat16).astype(jnp.float32)
+        pieces.append(piece)
+        value = value - piece
+    return pieces
+
+
 def cached_kernel(place_ref, packed_ref, cache_ref, partial_ref):
     group = packed_ref.shape[0]
-    rows = partial_ref.shape[1] - 8
+    rows = partial_ref.shape[1] - 16
     span = cache_ref.shape[0]
     live = place_ref[0] - place_ref[1] * span
     places = lax.broadcasted_iota(jnp.int32, (1, span), 1)
@@ -84,13 +92,18 @@
     out = jnp.dot(
         weights.astype(jnp.bfloat16), cache_ref[:, HD:], preferred_element_type=jnp.float32
     )
+    out = (out / total).astype(jnp.bfloat16)
     for head in range(group):
         at = slice(head * rows, (head + 1) * rows)
         partial_ref[head, pl.ds(0, rows)] = out[at]
-        peaks = jnp.broadcast_to(peak[at], (rows, HD)).T
-        totals = jnp.broadcast_to(total[at], (rows, HD)).T
-        partial_ref[head, pl.ds(rows, 4)] = peaks[:4]
-        partial_ref[head, pl.ds(rows + 4, 4)] = totals[:4]
+        peaks = jnp.broadcast_to(peak[at], (rows, HD)).T[:8]
+        totals = jnp.broadcast_to(total[at], (rows, HD)).T[:8]
+        lanes = lax.broadcasted_iota(jnp.int32, (16, rows), 0)
+        table = jnp.zeros((16, rows), jnp.float32)
+        for at_row, piece in enumerate(thirds(peaks) + thirds(totals)):
+            both = jnp.concatenate([piece, piece], axis=0)
+            table = jnp.where(lanes == at_row, both, table)
+        partial_ref[head, pl.ds(rows, 16)] = table.astype(jnp.bfloat16)
 
 
 def finish_kernel(second, *refs):
@@ -100,18 +113,17 @@
     else:
         (y_ref, new_ref) = refs[6:]
     group = packed_ref.shape[0]
-    rows = partial_ref.shape[1] - 8
-    columns = (packed_ref.shape[1] - rows) // 2
+    rows = partial_ref.shape[1] - 16
+    columns = packed_ref.shape[1] - rows
     queries = packed_ref[place_ref[1], pl.ds(0, rows), :]
     keyval = jnp.concatenate(
         [
             packed_ref[peer, pl.ds(rows, columns), :].astype(jnp.float32)
-            + packed_ref[peer, pl.ds(rows + columns, columns), :].astype(jnp.float32)
             for peer in range(group)
         ],
         axis=0,
     ).T
-    keys = turned(keyval[:, :HD], cos_ref[...], sin_ref[...]).astype(jnp.bfloat16)
+    keys = turned(keyval[:, :HD], cos_ref, sin_ref, int(second)).astype(jnp.bfloat16)
     values = keyval[:, HD:].astype(jnp.bfloat16)
     row_ids = lax.broadcasted_iota(jnp.int32, (rows, rows), 0)
     key_ids = lax.broadcasted_iota(jnp.int32, (rows, rows), 1)
@@ -127,8 +139,9 @@
     peak = jnp.broadcast_to(jnp.max(peaks, axis=1, keepdims=True), (rows, HD))
     stats = []
     for peer in range(group):
-        part_peak = jnp.broadcast_to(partial_ref[peer, pl.ds(rows, 1)], (HD, rows)).T
-        part_total = jnp.broadcast_to(partial_ref[peer, pl.ds(rows + 4, 1)], (HD, rows)).T
+        table = partial_ref[peer, pl.ds(rows, 16)].astype(jnp.float32)
+        part_peak = jnp.broadcast_to(table[0:1] + table[1:2] + table[2:3], (HD, rows)).T
+        part_total = jnp.broadcast_to(table[3:4] + table[4:5] + table[5:6], (HD, rows)).T
         peak = jnp.maximum(peak, part_peak)
         stats.append((part_peak, part_total))
     total = jnp.zeros((rows, HD), jnp.float32)
@@ -140,15 +153,25 @@
             weights.astype(jnp.bfloat16), value_rows, preferred_element_type=jnp.float32
         )
     for peer, (part_peak, part_total) in enumerate(stats):
-        shrink = jnp.exp(part_peak - peak)
-        total = total + shrink * part_total
-        out = out + shrink * partial_ref[peer, pl.ds(0, rows)]
+        shrink = jnp.exp(part_peak - peak) * part_total
+        total = total + shrink
+        out = out + shrink * partial_ref[peer, pl.ds(0, rows)].astype(jnp.float32)
     attended = (out / total).astype(jnp.bfloat16)
     chunks, _, part = y_ref.shape
     for c in range(chunks):
         y_ref[c] = jnp.dot(
             attended, wout_ref[:, pl.ds(c * part, part)], preferred_element_type=jnp.float32
         ).astype(jnp.bfloat16)
+
+
+def reduce_kernel(parts_ref, own_ref, full_ref, *short_ref):
+    summed = parts_ref[0].astype(jnp.float32)
+    for c in range(1, parts_ref.shape[0]):
+        summed = summed + parts_ref[c].astype(jnp.float32)
+    summed = own_ref[...].astype(jnp.float32) + summed
+    full_ref[...] = summed
+    if short_ref:
+        short_ref[0][...] = summed.astype(jnp.bfloat16)
 
 
 def local(slices, new_slice, norm_gain, w_query, w_keyval, w_out, cached_rows, lengths):
@@ -163,7 +186,8 @@
     )
     gain = norm_gain[0].reshape(head_count, 1, part)
 
-    place = jnp.stack([lengths[0], lax.axis_index("head") % group])
+    head_index = lax.axis_index("head")
+    place = jnp.stack([lengths[0], head_index % group, head_index])
     keyval_weights = w_keyval[0].T
 
     def gathered(own):
@@ -172,20 +196,21 @@
         )
 
     def partial_outputs(everything, turn, earlier):
-        cos = cosines[turn * rows : (turn + 1) * rows]
-        sin = sines[turn * rows : (turn + 1) * rows]
-        packed = pl.pallas_call(
-            project_kernel,
-            out_shape=jax.ShapeDtypeStruct((group, rows + 2 * key_columns, HD), jnp.bfloat16),
+        packed, own = pl.pallas_call(
+            functools.partial(project_kernel, turn),
+            out_shape=(
+                jax.ShapeDtypeStruct((group, rows + key_columns, HD), jnp.bfloat16),
+                jax.ShapeDtypeStruct((rows, part), jnp.bfloat16),
+            ),
             in_specs=[SMEM] + [VMEM] * 6,
-            out_specs=VMEM,
+            out_specs=(VMEM, VMEM),
             compiler_params=PARAMS,
             name=f"project{turn}",
-        )(place, everything, gain, w_query[0], keyval_weights, cos, sin)
+        )(place, everything, gain, w_query[0], keyval_weights, cosines, sines)
         packed = lax.all_to_all(packed, "head", 0, 0, axis_index_groups=groups)
         partial = pl.pallas_call(
             cached_kernel,
-            out_shape=jax.ShapeDtypeStruct((group, rows + 8, HD), jnp.float32),
+            out_shape=jax.ShapeDtypeStruct((group, rows + 16, HD), jnp.bfloat16),
             in_specs=[SMEM, VMEM, VMEM],
             out_specs=VMEM,
             compiler_params=PARAMS,
@@ -202,21 +227,30 @@
             out_specs=tuple([VMEM] * len(outputs)),
             compiler_params=PARAMS,
             name=f"finish{turn}",
-        )(place, packed, cos, sin, partial, w_out[0], *earlier)
-        return results[0], tuple(results[1:])
-
-    def reduced(partials):
-        arrived = lax.all_to_all(partials, "head", 0, 0)
-        return jnp.sum(arrived.astype(jnp.float32), axis=0)
-
-    partials, recent = partial_outputs(gathered(slices), 0, ())
-    first_out = slices.astype(jnp.float32) + reduced(partials)
+        )(place, packed, cosines, sines, partial, w_out[0], *earlier)
+        return results[0], own, tuple(results[1:])
+
+    def reduced(partials, own, turn):
+        outputs = [jax.ShapeDtypeStruct((rows, part), jnp.float32)]
+        if turn == 0:
+            outputs += [jax.ShapeDtypeStruct((rows, part), jnp.bfloat16)]
+        return pl.pallas_call(
+            reduce_kernel,
+            out_shape=tuple(outputs),
+            in_specs=[VMEM, VMEM],
+            out_specs=tuple([VMEM] * len(outputs)),
+            compiler_params=PARAMS,
+            name=f"reduce{turn}",
+        )(lax.all_to_all(partials, "head", 0, 0), own)
+
+    opening, place, cosines, sines = lax.optimization_barrier((slices, place, cosines, sines))
+    partials, own, recent = partial_outputs(gathered(opening), 0, ())
+    first_out, short = reduced(partials, own, 0)
     count = lax.axis_size("segment")
-    route = [(i, i + 1) for i in range(count - 1)]
-    arrived = lax.ppermute(first_out.astype(jnp.bfloat16), "segment", route)
+    arrived = lax.ppermute(short, "segment", [(i, i + 1) for i in range(count - 1)])
     entering = jnp.where(segment_index == 0, new_slice, arrived)
-    partials, _ = partial_outputs(gathered(entering), 1, recent)
-    second_out = entering.astype(jnp.float32) + reduced(partials)
+    partials, own, _ = partial_outputs(gathered(entering), 1, recent)
+    (second_out,) = reduced(partials, own, 1)
     return (first_out, second_out)
 
 

time: 140 us -> 136 us (0.971)
  blocking collectives: 93.1 us -> 114 us
  waiting for transfers between devices: 20 us -> 3.97 us
  starting transfers between devices: 9.07 us -> 1.91 us
  local copies, waits for them, and re-layouts: 2.73 us -> 0.52 us
  Pallas kernels: 10.1 us -> 11.8 us
    all_to_all x1 -> x2, blocking collectives: 21.5 us -> 45.3 us  [gathered(): lax.all_to_all(jnp.broadcast_to(own[None], (head_count, rows, part)), 'he...]
    all_to_all x1 -> x0, waiting for transfers between devices: 16.1 us -> none  [gathered(): lax.all_to_all(jnp.broadcast_to(own[None], (head_count, rows, part)), 'he...]
    all_to_all x1 -> x0, starting transfers between devices: 7.17 us -> none  [gathered(): lax.all_to_all(jnp.broadcast_to(own[None], (head_count, rows, part)), 'he...]
    broadcast_in_dim x2, local copies, waits for them, and re-layouts: 2 us -> 0.19 us  [gathered(): jnp.broadcast_to(own[None], (head_count, rows, part))]
    pallas_call x2 -> x4, Pallas kernels: 3.2 us -> 4.86 us  [the longest x2 3.23 us: partial_outputs(): pl.pallas_call(functools.partial(project_kernel, turn), out_shape=(jax.Sh...]
    all_to_all x2, blocking collectives: 18.2 us -> 16.8 us  [partial_outputs(): partial = lax.all_to_all(partial, 'head', 0, 0, axis_index_groups=groups)]
  transfers between devices with their start and end apart: 2 -> 1, of which waited for: 2 -> 1; matrix products, arithmetic and copies ran while one was open for 1% -> 0% of each run, Pallas kernels for 0% -> 0%
where the time goes in v3:
time: 136 us; the launch traced here: 135 us
  blocking collectives  114 us (84%)
  Pallas kernels  11.8 us (9%)
  waiting for transfers between devices  3.97 us (3%)
  starting transfers between devices  1.91 us (1%)
  other arithmetic  1.48 us (1%)
  between operations  1.43 us (1%)
    all_to_all x2, blocking collectives, gathered(): lax.all_to_all(jnp.broadcast_to(own[None], (head_count, rows, part)), 'he...  45.3 us
    all_to_all x2, blocking collectives, reduced(): lax.all_to_all(partials, 'head', 0, 0)  34.6 us
    all_to_all x2, blocking collectives, partial_outputs(): packed = lax.all_to_all(packed, 'head', 0, 0, axis_index_groups=groups)  17.5 us
    all_to_all x2, blocking collectives, partial_outputs(): partial = lax.all_to_all(partial, 'head', 0, 0, axis_index_groups=groups)  16.8 us
    ppermute x1, waiting for transfers between devices, local(): lax.ppermute(short, 'segment', [(i, i + 1) for i in range(count - 1)])  3.97 us
    pallas_call x2, Pallas kernels, partial_outputs(): pl.pallas_call(cached_kernel, out_shape=jax.ShapeDtypeStruct((group, rows...  3.9 us
    pallas_call x2, Pallas kernels, partial_outputs(): pl.pallas_call(functools.partial(project_kernel, turn), out_shape=(jax.Sh...  3.23 us
    pallas_call x2, Pallas kernels, partial_outputs(): pl.pallas_call(functools.partial(finish_kernel, bool(earlier)), out_shape...  3 us
  transfers between devices with their start and end apart: 1, of which 1 were waited for; matrix products, arithmetic and copies ran while one was open for 0% of the time, Pallas kernels for 0%

profile of v3, /device:TPU:96, one launch (start us, length us, event | category | flops | bytes accessed | tf_op | source)
XLA Modules:
  0.0 135.2 jit_solution(1305884880000775826)
XLA Ops:
  1.3 0.1 pad_add_fusion.place_ref.refs_0_
  1.4 0.5 multiply_sine_fusion
  1.9 0.3 copy-done.5
  2.2 0.1 broadcast_in_dim.4
  2.4 0.0 copy-start
  2.4 0.0 copy-start.2
  2.4 0.0 copy-start.4
  2.4 24.1 %all_to_all.40.x_ref = bf16[16,128,256]{2,1,0:T(8,128)(2,1)S(1)} all-to-all(bf16[16,128,256]{2,1,0:T(8,128)(2,1)S(1)} %broadcast_in_dim.4), channel_id=1, replica_groups=mesh['segment'=32,'head'=16] {'head'}, dimensions={0} | all-to-all | bytes 2097152 | tf_op jit(solution)/shard_map/all_to_all | solution.py:194
  26.5 0.0 copy-done
  26.5 0.0 copy-done.2
  26.5 0.0 copy-done.4
  26.5 0.0 copy-start.3
  26.5 1.6 %project0.1 = (bf16[4,192,128]{2,1,0:T(8,128)(2,1)S(1)}, bf16[128,256]{1,0:T(8,128)(2,1)S(1)}) custom-call(s32[3]{0:T(128)S(1)} %pad_add_fusion.place_ref.refs_0_, bf16[16,128,256]{2,1,0:T(8,128)(2,1)S(1)} %all_to_all.40.x_ref, f32[16,1,256]{2,1,0:T(1,128)S(1)} %bitcast.19, bf16[4096,128]{1,0:T(8,128)(2,1)S(1)} %bitcast.11, bf16[64,4096]{1,0:T(8,128)(2,1)S(1)} %bitcast.15, ...), custom_call_target="tpu_custom_call" | custom-call | tf_op jit(solution)/shard_map/project0/pallas_call | solution.py:199
  28.2 8.8 %all_to_all.41.packed_ref.refs_1_ = bf16[4,192,128]{2,1,0:T(8,128)(2,1)S(1)} all-to-all(bf16[4,192,128]{2,1,0:T(8,128)(2,1)S(1)} %get-tuple-element.18), channel_id=1, replica_groups={{0,1,2,3},{4,5,6,7},{8,9,10,11},{12,13,14,15},{16,17,18,19},{20,21,22,2..., dimensions={0} | all-to-all | bytes 393216 | tf_op jit(solution)/shard_map/all_to_all | solution.py:210
  37.0 0.0 copy-done.3
  37.0 1.9 %cached0.1 = bf16[4,144,128]{2,1,0:T(8,128)(2,1)S(1)} custom-call(s32[3]{0:T(128)S(1)} %pad_add_fusion.place_ref.refs_0_, bf16[4,192,128]{2,1,0:T(8,128)(2,1)S(1)} %all_to_all.41.packed_ref.refs_1_, bf16[1024,256]{1,0:T(8,128)(2,1)S(1)} %bitcast.17), custom_call_target="tpu_custom_call" | custom-call | tf_op jit(solution)/shard_map/cached0/pallas_call | solution.py:211
  38.9 8.4 %all_to_all.42.refs_4_ = bf16[4,144,128]{2,1,0:T(8,128)(2,1)S(1)} all-to-all(bf16[4,144,128]{2,1,0:T(8,128)(2,1)S(1)} %cached0.1), channel_id=1, replica_groups={{0,1,2,3},{4,5,6,7},{8,9,10,11},{12,13,14,15},{16,17,18,19},{20,21,22,2..., dimensions={0} | all-to-all | bytes 294912 | tf_op jit(solution)/shard_map/all_to_all | solution.py:219
  47.4 1.5 %finish0.1 = (bf16[16,128,256]{2,1,0:T(8,128)(2,1)S(1)}, bf16[2,128,128]{2,1,0:T(8,128)(2,1)S(1)}) custom-call(s32[3]{0:T(128)S(1)} %pad_add_fusion.place_ref.refs_0_, bf16[4,192,128]{2,1,0:T(8,128)(2,1)S(1)} %all_to_all.41.packed_ref.refs_1_, f32[256,64]{1,0:T(8,128)S(1)} %get-tuple-element.16.cos_ref.refs_2_, ...), custom_call_target="tpu_custom_call" | custom-call | tf_op jit(solution)/shard_map/finish0/pallas_call | solution.py:223
  48.9 16.8 %all_to_all.43.parts_ref = bf16[16,128,256]{2,1,0:T(8,128)(2,1)S(1)} all-to-all(bf16[16,128,256]{2,1,0:T(8,128)(2,1)S(1)} %get-tuple-element.19), channel_id=1, replica_groups=mesh['segment'=32,'head'=16] {'head'}, dimensions={0} | all-to-all | bytes 2097152 | tf_op jit(solution)/shard_map/all_to_all | solution.py:244
  65.6 0.8 reduce0.1
  66.5 1.9 %collective-permute-start = (bf16[128,256]{1,0:T(8,128)(2,1)}, bf16[128,256]{1,0:T(8,128)(2,1)}, u32[]{:S(2)}, u32[]{:S(2)}) collective-permute-start(bf16[128,256]{1,0:T(8,128)(2,1)} %get-tuple-element.22), channel_id=1, source_target_pairs={{0,16},{16,32},{32,48},{48,64},{64,80},{80,96},{96,112},{112,128},... | collective-permute-start | bytes 196616 | tf_op jit(solution)/shard_map/ppermute | solution.py:250
  68.4 4.0 %collective-permute-done = bf16[128,256]{1,0:T(8,128)(2,1)} collective-permute-done((bf16[128,256]{1,0:T(8,128)(2,1)}, bf16[128,256]{1,0:T(8,128)(2,1)}, u32[]{:S(2)}, u32[]{:S(2)}) %collective-permute-start) | collective-permute-done | bytes 65568 | tf_op jit(solution)/shard_map/ppermute | solution.py:250
  72.4 0.9 broadcast_select_fusion
  73.2 0.1 broadcast_in_dim.5
  73.3 21.2 %all_to_all.44.x_ref = bf16[16,128,256]{2,1,0:T(8,128)(2,1)S(1)} all-to-all(bf16[16,128,256]{2,1,0:T(8,128)(2,1)S(1)} %broadcast_in_dim.5), channel_id=1, replica_groups=mesh['segment'=32,'head'=16] {'head'}, dimensions={0} | all-to-all | bytes 2097152 | tf_op jit(solution)/shard_map/all_to_all | solution.py:194
  94.5 1.6 %project1.1 = (bf16[4,192,128]{2,1,0:T(8,128)(2,1)S(1)}, bf16[128,256]{1,0:T(8,128)(2,1)S(1)}) custom-call(s32[3]{0:T(128)S(1)} %pad_add_fusion.place_ref.refs_0_, bf16[16,128,256]{2,1,0:T(8,128)(2,1)S(1)} %all_to_all.44.x_ref, f32[16,1,256]{2,1,0:T(1,128)S(1)} %bitcast.20, bf16[4096,128]{1,0:T(8,128)(2,1)S(1)} %bitcast.12, bf16[64,4096]{1,0:T(8,128)(2,1)S(1)} %bitcast.16, ...), custom_call_target="tpu_custom_call" | custom-call | tf_op jit(solution)/shard_map/project1/pallas_call | solution.py:199
  96.1 8.7 %all_to_all.45.packed_ref.refs_1_ = bf16[4,192,128]{2,1,0:T(8,128)(2,1)S(1)} all-to-all(bf16[4,192,128]{2,1,0:T(8,128)(2,1)S(1)} %get-tuple-element.23), channel_id=1, replica_groups={{0,1,2,3},{4,5,6,7},{8,9,10,11},{12,13,14,15},{16,17,18,19},{20,21,22,2..., dimensions={0} | all-to-all | bytes 393216 | tf_op jit(solution)/shard_map/all_to_all | solution.py:210
  104.8 1.9 %cached1.1 = bf16[4,144,128]{2,1,0:T(8,128)(2,1)S(1)} custom-call(s32[3]{0:T(128)S(1)} %pad_add_fusion.place_ref.refs_0_, bf16[4,192,128]{2,1,0:T(8,128)(2,1)S(1)} %all_to_all.45.packed_ref.refs_1_, bf16[1024,256]{1,0:T(8,128)(2,1)S(1)} %bitcast.18), custom_call_target="tpu_custom_call" | custom-call | tf_op jit(solution)/shard_map/cached1/pallas_call | solution.py:211
  106.7 8.4 %all_to_all.46.refs_4_ = bf16[4,144,128]{2,1,0:T(8,128)(2,1)S(1)} all-to-all(bf16[4,144,128]{2,1,0:T(8,128)(2,1)S(1)} %cached1.1), channel_id=1, replica_groups={{0,1,2,3},{4,5,6,7},{8,9,10,11},{12,13,14,15},{16,17,18,19},{20,21,22,2..., dimensions={0} | all-to-all | bytes 294912 | tf_op jit(solution)/shard_map/all_to_all | solution.py:219
  115.1 1.5 %finish1.1 = bf16[16,128,256]{2,1,0:T(8,128)(2,1)S(1)} custom-call(s32[3]{0:T(128)S(1)} %pad_add_fusion.place_ref.refs_0_, bf16[4,192,128]{2,1,0:T(8,128)(2,1)S(1)} %all_to_all.45.packed_ref.refs_1_, f32[256,64]{1,0:T(8,128)S(1)} %get-tuple-element.16.cos_ref.refs_2_, f32[256,64]{1,0:T(8,128)S(1)} %get-tuple-element.17.sin_ref.refs_3_, ...), custom_call_target="tpu_custom_call" | custom-call | tf_op jit(solution)/shard_map/finish1/pallas_call | solution.py:223
  116.6 17.8 %all_to_all.47.parts_ref = bf16[16,128,256]{2,1,0:T(8,128)(2,1)S(1)} all-to-all(bf16[16,128,256]{2,1,0:T(8,128)(2,1)S(1)} %finish1.1), channel_id=1, replica_groups=mesh['segment'=32,'head'=16] {'head'}, dimensions={0} | all-to-all | bytes 2097152 | tf_op jit(solution)/shard_map/all_to_all | solution.py:244
  134.4 0.8 reduce1.1
  (5 shorter events, 0.0 us)
Async XLA Ops:
  1.4 0.8 copy-start.5
  2.4 24.2 %copy-start = (bf16[1,4096,128]{2,1,0:T(8,128)(2,1)S(1)}, bf16[1,4096,128]{2,1,0:T(8,128)(2,1)}, u32[]{:S(2)}) copy-start(bf16[1,4096,128]{2,1,0:T(8,128)(2,1)} %param.11) | copy-start | bytes 3145732
  2.4 24.1 %copy-start.2 = (bf16[1,4096,64]{1,2,0:T(8,128)(2,1)S(1)}, bf16[1,4096,64]{1,2,0:T(8,128)(2,1)}, u32[]{:S(2)}) copy-start(bf16[1,4096,64]{1,2,0:T(8,128)(2,1)} %param.12) | copy-start | bytes 1572868
  2.4 24.1 %copy-start.4 = (f32[1,4096]{1,0:T(1,128)S(1)}, f32[1,4096]{1,0:T(1,128)}, u32[]{:S(2)}) copy-start(f32[1,4096]{1,0:T(1,128)} %param.10) | copy-start | bytes 49156
  26.5 10.5 %copy-start.3 = (bf16[1,1024,256]{2,1,0:T(8,128)(2,1)S(1)}, bf16[1,1024,256]{2,1,0:T(8,128)(2,1)}, u32[]{:S(2)}) copy-start(bf16[1,1024,256]{2,1,0:T(8,128)(2,1)} %param.14) | copy-start | bytes 1572868
  28.1 19.2 %copy-start.1 = (bf16[1,128,4096]{2,1,0:T(8,128)(2,1)S(1)}, bf16[1,128,4096]{2,1,0:T(8,128)(2,1)}, u32[]{:S(2)}) copy-start(bf16[1,128,4096]{2,1,0:T(8,128)(2,1)} %param.13) | copy-start | bytes 3145732
  66.5 5.9 %collective-permute-start = (bf16[128,256]{1,0:T(8,128)(2,1)}, bf16[128,256]{1,0:T(8,128)(2,1)}, u32[]{:S(2)}, u32[]{:S(2)}) collective-permute-start(bf16[128,256]{1,0:T(8,128)(2,1)} %get-tuple-element.22), channel_id=1, source_target_pairs={{0,16},{16,32},{32,48},{48,64},{64,80},{80,96},{96,112},{112,128},... | collective-permute-start | bytes 196616 | tf_op jit(solution)/shard_map/ppermute | solution.py:250
